TPU v7x, 32 devices: a whole 2x2x4 slice. The times are simulated.
32 devices in a mesh: row: 4 (over y, x), col: 8 (over z, core).
Axes of the slice: x: 2, y: 2, z: 4, core: 2. Of those that a mesh axis runs over, the one named last changes fastest.
Arguments:
- ancestor_inverse: float32 [24576, 24576], P('row', 'col'), may hold values from -0.0546875 to 0.0546875
- lower_panel: float32 [2, 24576, 256], P(None, ('row', 'col')), may hold values from -6 to 6
- diag_factor: float32 [2, 256, 256], replicated, may hold values from -0.09375 to 0.09375
- diag_block: float32 [2, 256, 256], replicated, may hold values from -24 to 24
- pattern: int32 [2, 384], replicated, may hold values 0 or 1
Outputs:
- panel_inverse: float32 [2, 24576, 256], P(None, ('row', 'col'))
- diag_inverse: float32 [2, 256, 256], replicated
All inputs are finite; a program needn't handle non-finite values.
Results may differ from a plain program's by a relative error of at most 0.000071.
Values sent between devices are 32-bit elements; how exact they have to be, the bound alone decides.
A program may use at most 192 MiB of HBM per device.

v0:
```python
import jax
import jax.numpy as jnp
from jax import lax
from jax.sharding import PartitionSpec as P

BS = 64
NS = 2


HIGHEST_PREC = lax.Precision.HIGHEST


def from_root(block, axis, owner):
    block = jnp.where(lax.axis_index(axis) == owner, block, jnp.zeros_like(block))
    return lax.psum(block, axis)


def mask_rows(pattern_part, row_start, length):
    blocks = lax.dynamic_slice_in_dim(pattern_part, row_start // BS, length // BS, 1)
    return jnp.repeat(blocks, BS, axis=1).astype(jnp.float32)


def local(ancestor_inverse, lower_panel, diag_factor, diag_block, pattern):
    row_count = lax.axis_size("row")
    col_count = lax.axis_size("col")
    row_index = lax.axis_index("row")
    col_index = lax.axis_index("col")
    piece_rows = lower_panel.shape[1]
    strip_cols = ancestor_inverse.shape[1]
    piece_start = (row_index * col_count + col_index) * piece_rows
    panel_list = []
    diag_list = []
    for snode in range(NS):
        local_mask = mask_rows(pattern[snode : snode + 1], piece_start, piece_rows)
        normed = (
            jnp.einsum(
                "spw,swv->spv",
                lower_panel[snode : snode + 1],
                diag_factor[snode : snode + 1],
                precision=HIGHEST_PREC,
            )
            * local_mask[:, :, None]
        )
        gathered = lax.all_gather(normed, "col", axis=1, tiled=True)
        ratio = col_count // row_count
        offset = col_index % ratio * strip_cols
        selected = lax.dynamic_slice_in_dim(gathered, offset, strip_cols, 1)
        root_row = col_index * row_count // col_count
        transposed = from_root(selected, "row", root_row)
        shares = lax.psum_scatter(
            -jnp.einsum("ij,sjw->isw", ancestor_inverse, transposed, precision=HIGHEST_PREC),
            "col",
            scatter_dimension=0,
            tiled=True,
        )
        panel_result = jnp.transpose(shares, (1, 0, 2)) * local_mask[:, :, None]
        partial_value = jnp.einsum("spw,spv->swv", normed, panel_result, precision=HIGHEST_PREC)
        update = lax.psum(partial_value, ("row", "col"))
        diag_one = diag_block[snode : snode + 1] - update
        panel_list.append(panel_result)
        diag_list.append(diag_one)
    panel_inverse = jnp.concatenate(panel_list, axis=0)
    diag_inverse = jnp.concatenate(diag_list, axis=0)
    return (panel_inverse, diag_inverse)


def solution(mesh):
    return jax.shard_map(
        local,
        mesh=mesh,
        in_specs=(P("row", "col"), P(None, ("row", "col"), None), P(), P(), P()),
        out_specs=(P(None, ("row", "col"), None), P()),
        check_vma=False,
    )
```

profile of v0, /device:TPU:0, one launch (start us, length us, event | category | flops | bytes accessed | tf_op | source)
XLA Modules:
  0.0 764.9 jit_solution(5222050702606410304)
XLA Ops:
  7.2 0.8 fusion.20
  8.1 0.1 fusion.17
  8.1 0.1 broadcast_in_dim.5
  8.2 0.1 convert_element_type.37
  8.3 2.9 convolution_multiply_fusion
  11.2 0.0 all-gather.5.cloned.1.call-start
  11.2 0.1 broadcast_in_dim.4
  11.3 0.1 convert_element_type.34
  11.4 2.6 convolution_multiply_fusion.1
  14.0 0.0 all-reduce.7.cloned.1.call-start
  14.1 64.6 %all-gather.7.cloned.1.call-done = f32[6144,256]{1,0:T(8,128)} async-done(((f32[768,256]{1,0:T(8,128)}), f32[6144,256]{1,0:T(8,128)}) %all-gather.7.cloned.1.call-update) | async-done | bytes 6291472 | tf_op jit(solution)/shard_map/all_gather | solution.py:44
  78.7 3.7 dynamic-slice_select_fusion
  82.5 61.3 %all-gather.5.cloned.1.call-done = f32[6144,256]{1,0:T(8,128)} async-done(((f32[768,256]{1,0:T(8,128)}), f32[6144,256]{1,0:T(8,128)}) %all-gather.5.cloned.1.call-update) | async-done | bytes 6291472 | tf_op jit(solution)/shard_map/all_gather | solution.py:44
  143.7 3.8 dynamic-slice_select_fusion.1
  147.5 0.0 reduce-scatter.5.cloned.1.call-start
  147.6 136.9 %all-reduce.7.cloned.1.call-done = (f32[3072,256]{1,0:T(8,128)}, f32[3072,256]{1,0:T(8,128)}) async-done(((f32[3072,256]{1,0:T(8,128)}, f32[3072,256]{1,0:T(8,128)}), (f32[3072,256]{1,0:T(8,128)}, f32[3072,256]{1,0:T(8,128)})) %all-reduce.7.cloned.1.call-update) | async-done | bytes 6291472 | tf_op jit(solution)/shard_map/psum | solution.py:15
  284.5 140.1 %fusion.1 = f32[6144,1,256]{0,2,1:T(8,128)} fusion(f32[3072,256]{1,0:T(8,128)} %get-tuple-element.6, f32[6144,3072]{1,0:T(8,128)} %param.5), kind=kOutput, calls=%fused_computation.3 | convolution fusion | flops 57983631360 | bytes 84934656 | tf_op jit(solution)/shard_map/ij,sjw->isw/dot_general | solution.py:51
  424.6 0.0 reduce-scatter.3.cloned.1.call-start
  424.7 1.8 copy-done.2
  426.5 126.0 %fusion = f32[6144,1,256]{0,2,1:T(8,128)} fusion(f32[3072,256]{1,0:T(8,128)S(1)} %copy-done.2, f32[6144,3072]{1,0:T(8,128)} %param.5), kind=kOutput, calls=%fused_computation.2 | convolution fusion | flops 57983631360 | bytes 84934656 | tf_op jit(solution)/shard_map/ij,sjw->isw/dot_general | solution.py:51
  552.6 0.0 all-reduce.5.cloned.1.call-start
  552.7 1.0 copy-done
  553.7 3.3 convolution_bitcast_fusion
  557.0 65.2 %reduce-scatter.3.cloned.1.call-done = f32[768,1,256]{0,2,1:T(8,128)} async-done(((f32[6144,1,256]{0,2,1:T(8,128)}), f32[768,1,256]{0,2,1:T(8,128)}) %reduce-scatter.3.cloned.1.call-update) | async-done | bytes 786448 | tf_op jit(solution)/shard_map/reduce_scatter | solution.py:50
  622.1 3.3 convolution_bitcast_fusion.1
  625.5 0.1 bitcast_multiply_fusion
  625.6 0.1 bitcast_multiply_fusion.1
  625.7 0.1 pad_maximum_fusion
  625.8 1.6 copy.7
  627.4 128.5 %all-reduce.5.cloned.1.call-done = (f32[1,256,256]{2,1,0:T(8,128)}, f32[1,256,256]{2,1,0:T(8,128)}) async-done(((f32[1,256,256]{2,1,0:T(8,128)}, f32[1,256,256]{2,1,0:T(8,128)}), (f32[1,256,256]{2,1,0:T(8,128)}, f32[1,256,256]{2,1,0:T(8,128)})) %all-reduce.5.cloned.1.call-update) | async-done | bytes 524304 | tf_op jit(solution)/shard_map/psum | solution.py:58
  755.9 1.1 slice_subtract_fusion.1
  757.0 0.8 pad_maximum_fusion.1
  (20 shorter events, 0.2 us)
Async XLA Ops:
  7.2 4.2 copy-start.5
  7.2 71.6 %all-gather.7.cloned.1.call-start = ((), (), s32[]{:S(2)}) async-start(), calls=%async_computation.5 | async-start | bytes 7077888 | tf_op jit(solution)/shard_map/all_gather | solution.py:44
  11.2 132.6 %all-gather.5.cloned.1.call-start = ((), (), s32[]{:S(2)}) async-start(), calls=%async_computation.4 | async-start | bytes 7077888 | tf_op jit(solution)/shard_map/all_gather | solution.py:44
  14.0 270.5 %all-reduce.7.cloned.1.call-start = ((), (), s32[]{:S(2)}) async-start(), calls=%async_computation.7 | async-start | bytes 12582912 | tf_op jit(solution)/shard_map/psum | solution.py:15
  147.5 405.1 %reduce-scatter.5.cloned.1.call-start = ((), (), s32[]{:S(2)}) async-start(), calls=%async_computation.3 | async-start | bytes 7077888 | tf_op jit(solution)/shard_map/reduce_scatter | solution.py:50
  424.6 1.9 copy-start.2
  424.6 197.5 %reduce-scatter.3.cloned.1.call-start = ((), (), s32[]{:S(2)}) async-start(), calls=%async_computation.2 | async-start | bytes 7077888 | tf_op jit(solution)/shard_map/reduce_scatter | solution.py:50
  552.5 1.1 copy-start
  552.5 69.6 %copy-start.1 = (f32[768,256]{1,0:T(8,128)S(1)}, f32[768,256]{1,0:T(8,128)}, u32[]{:S(2)}) copy-start(f32[768,256]{1,0:T(8,128)} %convolution_multiply_fusion.1) | copy-start | bytes 2359300
  552.6 203.3 %all-reduce.5.cloned.1.call-start = ((), (), s32[]{:S(2)}) async-start(), calls=%async_computation.6 | async-start | bytes 1048576 | tf_op jit(solution)/shard_map/psum | solution.py:58
  553.7 71.8 %copy-start.3 = (f32[768,1,256]{0,2,1:T(8,128)S(1)}, f32[768,1,256]{0,2,1:T(8,128)}, u32[]{:S(2)}) copy-start(f32[768,1,256]{0,2,1:T(8,128)} %reduce-scatter.5.cloned.1.call-done) | copy-start | bytes 2359300
  622.1 3.4 copy-start.4
  625.6 130.2 %copy-start.6 = (f32[2,256,256]{2,1,0:T(8,128)S(1)}, f32[2,256,256]{2,1,0:T(8,128)}, u32[]{:S(2)}) copy-start(f32[2,256,256]{2,1,0:T(8,128)} %param.8) | copy-start | bytes 1572868
Sparse Core Ops, SparseCore 0:
  11.3 67.4 all-gather.6
  80.4 63.3 all-gather.4
  147.6 136.7 all-reduce.6
  424.7 69.7 reduce-scatter.4
  552.7 69.3 reduce-scatter.2
  628.0 127.7 all-reduce.4
where the time goes:
time: 768 us; the launch traced here: 765 us
  waiting for transfers between devices  457 us (60%)
  matrix products  278 us (36%)
  between operations  14.5 us (2%)
  other arithmetic  9.7 us (1%)
    dot_general x2, matrix products, local(): jnp.einsum('ij,sjw->isw', ancestor_inverse, transposed, precision=HIGHEST...  266 us
    psum x1, waiting for transfers between devices, from_root(): return lax.psum(block, axis)  137 us
    psum x1, waiting for transfers between devices, local(): update = lax.psum(partial_value, ('row', 'col'))  128 us
    all_gather x2, waiting for transfers between devices, local(): gathered = lax.all_gather(normed, 'col', axis=1, tiled=True)  126 us
    reduce_scatter x2, waiting for transfers between devices, local(): lax.psum_scatter(-jnp.einsum('ij,sjw->isw', ancestor_inverse, transposed,...  65.2 us
  transfers between devices with their start and end apart: 6, of which 5 were waited for; matrix products, arithmetic and copies ran while one was open for 18% of the time, Pallas kernels for 0%

commit v1 on v0

v1 whole, which is shorter than its diff:
```python
import jax
import jax.numpy as jnp
from jax import lax
from jax.sharding import PartitionSpec as P

HIGHEST_PREC = lax.Precision.HIGHEST
HIGH_PREC = lax.Precision.HIGH


def local(ancestor_inverse, lower_panel, diag_factor, diag_block, pattern):
    row_count = lax.axis_size("row")
    col_count = lax.axis_size("col")
    row_index = lax.axis_index("row")
    col_index = lax.axis_index("col")
    snodes, piece_rows, width = lower_panel.shape
    tile_rows = row_count * col_count * piece_rows // pattern.shape[1]
    piece_start = (row_index * col_count + col_index) * piece_rows
    blocks = lax.dynamic_slice_in_dim(pattern, piece_start // tile_rows, piece_rows // tile_rows, 1)
    mask = jnp.repeat(blocks, tile_rows, axis=1).astype(jnp.float32)[:, :, None]
    normed = (
        jnp.einsum("spw,swv->spv", lower_panel, diag_factor, precision=HIGHEST_PREC) * mask
    )
    part_rows = piece_rows // row_count
    parts = normed.reshape(snodes, row_count, part_rows, width)
    number = (row_index * col_count + col_index) % row_count
    strips = []
    for snode in range(snodes):
        rounds = []
        for step in range(row_count):
            pairs = []
            for r in range(row_count):
                for c in range(col_count):
                    piece = r * col_count + c
                    q = (piece % row_count + step) % row_count
                    pairs.append((piece, q * col_count + piece // row_count))
            block = lax.dynamic_index_in_dim(parts[snode], (number + step) % row_count, 0, False)
            rounds.append(lax.ppermute(block, ("row", "col"), pairs))
        order = (row_index - jnp.arange(row_count)) % row_count
        received = jnp.take(jnp.stack(rounds), order, axis=0)
        everything = lax.all_gather(received, "row", axis=0)
        strips.append(jnp.swapaxes(everything, 0, 1).reshape(row_count * piece_rows, width))
    panels = []
    for snode in range(snodes):
        product = jnp.dot(ancestor_inverse, strips[snode], precision=HIGH_PREC)
        share = lax.psum_scatter(product, "col", scatter_dimension=0, tiled=True)
        panels.append(-share * mask[snode])
    panel_inverse = jnp.stack(panels)
    partial = jnp.einsum("spw,spv->swv", normed, panel_inverse, precision=HIGHEST_PREC)
    diag_inverse = diag_block - lax.psum(partial, ("row", "col"))
    return panel_inverse, diag_inverse


def solution(mesh):
    return jax.shard_map(
        local,
        mesh=mesh,
        in_specs=(P("row", "col"), P(None, ("row", "col"), None), P(), P(), P()),
        out_specs=(P(None, ("row", "col"), None), P()),
        check_vma=False,
    )
```

time: 768 us -> 534 us (0.70)
  waiting for transfers between devices: 457 us -> 313 us
  matrix products: 278 us -> 147 us
  starting transfers between devices: 0.25 us -> 25.1 us
  local copies, waits for them, and re-layouts: 5.56 us -> 20.7 us
    psum x2 -> x1, waiting for transfers between devices: 265 us -> 125 us  [local(): diag_inverse = diag_block - lax.psum(partial, ('row', 'col'))]
    dot_general x6 -> x4, matrix products: 278 us -> 147 us  [the longest x2 140 us: local(): product = jnp.dot(ancestor_inverse, strips[snode], precision=HIGH_PREC)]
    all_gather x2, waiting for transfers between devices: 126 us -> 46.5 us  [local(): everything = lax.all_gather(received, 'row', axis=0)]
    ppermute x0 -> x8, waiting for transfers between devices: none -> 74 us  [local(): rounds.append(lax.ppermute(block, ('row', 'col'), pairs))]
    ppermute x0 -> x8, starting transfers between devices: none -> 24.9 us  [local(): rounds.append(lax.ppermute(block, ('row', 'col'), pairs))]
    another operation x0 -> x5, other arithmetic: none -> 7.83 us  [the longest x3 4.75 us: local(): panel_inverse = jnp.stack(panels)]
  transfers between devices with their start and end apart: 6 -> 13, of which waited for: 5 -> 7; matrix products, arithmetic and copies ran while one was open for 18% -> 30% of each run, Pallas kernels for 0% -> 0%
where the time goes in v1:
time: 534 us
  waiting for transfers between devices  313 us (59%)
  matrix products  147 us (28%)
  starting transfers between devices  25.1 us (5%)
  local copies, waits for them, and re-layouts  20.7 us (4%)
  between operations  14 us (3%)
  other arithmetic  13.6 us (3%)
    dot_general x2, matrix products, local(): product = jnp.dot(ancestor_inverse, strips[snode], precision=HIGH_PREC)  140 us
    psum x1, waiting for transfers between devices, local(): diag_inverse = diag_block - lax.psum(partial, ('row', 'col'))  125 us
    ppermute x8, waiting for transfers between devices, local(): rounds.append(lax.ppermute(block, ('row', 'col'), pairs))  74 us
    reduce_scatter x2, waiting for transfers between devices, local(): share = lax.psum_scatter(product, 'col', scatter_dimension=0, tiled=True)  67.4 us
    all_gather x2, waiting for transfers between devices, local(): everything = lax.all_gather(received, 'row', axis=0)  46.5 us
    ppermute x8, starting transfers between devices, local(): rounds.append(lax.ppermute(block, ('row', 'col'), pairs))  24.9 us
  transfers between devices with their start and end apart: 13, of which 7 were waited for; matrix products, arithmetic and copies ran while one was open for 30% of the time, Pallas kernels for 0%

profile of v1, /device:TPU:0, one launch (start us, length us, event | category | flops | bytes accessed | tf_op | source)
XLA Modules:
  0.0 533.6 jit_solution(12290840376613704863)
XLA Ops:
  8.6 2.5 convolution_multiply_fusion
  11.1 1.2 fusion.3
  12.4 1.3 dynamic-slice_bitcast_fusion.3
  14.3 7.7 %collective-permute-start.5 = (f32[192,256]{1,0:T(8,128)S(1)}, f32[192,256]{1,0:T(8,128)S(1)}, u32[]{:S(2)}, u32[]{:S(2)}) collective-permute-start(f32[192,256]{1,0:T(8,128)S(1)} %get-tuple-element.20), channel_id=1, source_target_pairs={{0,8},{1,16},{2,24},{3,0},{4,9},{5,17},{6,25},{7,1},{8,10},{9,18},... | collective-permute-start | bytes 589832 | tf_op jit(solution)/shard_map/ppermute | solution.py:37
  22.0 2.0 collective-permute-start.6
  24.0 5.0 collective-permute-start.7
  29.0 2.0 dynamic-slice_bitcast_fusion.7
  31.0 3.0 collective-permute-start
  34.1 4.7 collective-permute-start.1
  38.7 45.7 %collective-permute-done.5 = f32[192,256]{1,0:T(8,128)S(1)} collective-permute-done((f32[192,256]{1,0:T(8,128)S(1)}, f32[192,256]{1,0:T(8,128)S(1)}, u32[]{:S(2)}, u32[]{:S(2)}) %collective-permute-start.5) | collective-permute-done | bytes 196640 | tf_op jit(solution)/shard_map/ppermute | solution.py:37
  84.5 16.8 %collective-permute-done.6 = f32[192,256]{1,0:T(8,128)S(1)} collective-permute-done((f32[192,256]{1,0:T(8,128)S(1)}, f32[192,256]{1,0:T(8,128)S(1)}, u32[]{:S(2)}, u32[]{:S(2)}) %collective-permute-start.6) | collective-permute-done | bytes 196640 | tf_op jit(solution)/shard_map/ppermute | solution.py:37
  101.3 1.9 collective-permute-start.3
  103.2 0.9 pad_maximum_fusion.2
  104.2 2.6 gather_fusion.1
  106.8 7.3 %collective-permute-done.1 = f32[192,256]{1,0:T(8,128)} collective-permute-done((f32[192,256]{1,0:T(8,128)}, f32[192,256]{1,0:T(8,128)}, u32[]{:S(2)}, u32[]{:S(2)}) %collective-permute-start.1) | collective-permute-done | bytes 196640 | tf_op jit(solution)/shard_map/ppermute | solution.py:37
  114.1 4.2 collective-permute-done.2
  118.2 2.1 pad_maximum_fusion.1
  120.4 2.7 gather_fusion
  123.1 2.8 broadcast_select_fusion.1
  126.7 46.5 %all-gather.5.cloned.1.call-done = f32[16,192,256]{2,1,0:T(8,128)} async-done(((f32[4,192,256]{2,1,0:T(8,128)}), f32[16,192,256]{2,1,0:T(8,128)}) %all-gather.5.cloned.1.call-update) | async-done | bytes 3145744 | tf_op jit(solution)/shard_map/all_gather | solution.py:40
  173.1 3.8 copy.18
  177.0 69.9 %convolution_bitcast_fusion.1 = f32[6144,256]{0,1:T(8,128)} fusion(f32[3072,256]{1,0:T(8,128)} %bitcast.53, f32[6144,3072]{1,0:T(8,128)} %param.7), kind=kOutput, calls=%fused_computation.3 | convolution fusion | flops 28991029248 | bytes 84934656 | tf_op jit(solution)/shard_map/dot_general | solution.py:44
  247.0 3.8 copy.19
  250.8 69.9 %convolution_bitcast_fusion = f32[6144,256]{0,1:T(8,128)} fusion(f32[3072,256]{1,0:T(8,128)} %bitcast.54, f32[6144,3072]{1,0:T(8,128)} %param.7), kind=kOutput, calls=%fused_computation.2 | convolution fusion | flops 28991029248 | bytes 84934656 | tf_op jit(solution)/shard_map/dot_general | solution.py:44
  321.0 2.1 multiply_bitcast_fusion.1
  323.1 67.4 %reduce-scatter.5.cloned.1.call-done = f32[768,256]{0,1:T(8,128)} async-done(((f32[6144,256]{0,1:T(8,128)}), f32[768,256]{0,1:T(8,128)}) %reduce-scatter.5.cloned.1.call-update) | async-done | bytes 786448 | tf_op jit(solution)/shard_map/reduce_scatter | solution.py:45
  390.6 1.2 multiply_bitcast_fusion
  392.6 4.6 fusion.2
  397.3 1.5 pad_maximum_fusion
  398.8 1.6 copy.22
  400.4 124.6 %all-reduce.2.cloned.1.call-done = f32[2,256,256]{2,1,0:T(8,128)} async-done(((f32[2,256,256]{2,1,0:T(8,128)}), f32[2,256,256]{2,1,0:T(8,128)}) %all-reduce.2.cloned.1.call-update) | async-done | bytes 524304 | tf_op jit(solution)/shard_map/psum | solution.py:49
  525.0 2.1 sub.18
  (33 shorter events, 4.1 us)
Async XLA Ops:
  7.2 1.4 copy-start
  7.2 166.0 %all-gather.5.cloned.1.call-start = ((), (), s32[]{:S(2)}) async-start(), calls=%async_computation.5 | async-start | bytes 3932160 | tf_op jit(solution)/shard_map/all_gather | solution.py:40
  13.7 20.4 %collective-permute-start.4 = (f32[192,256]{1,0:T(8,128)S(1)}, f32[192,256]{1,0:T(8,128)S(1)}, u32[]{:S(2)}, u32[]{:S(2)}) collective-permute-start(f32[192,256]{1,0:T(8,128)S(1)} %get-tuple-element.17), channel_id=1, source_target_pairs={{0,0},{1,8},{2,16},{3,24},{4,1},{5,9},{6,17},{7,25},{8,2},{9,10},{... | collective-permute-start | bytes 589832 | tf_op jit(solution)/shard_map/ppermute | solution.py:37
  14.3 70.1 %collective-permute-start.5 = (f32[192,256]{1,0:T(8,128)S(1)}, f32[192,256]{1,0:T(8,128)S(1)}, u32[]{:S(2)}, u32[]{:S(2)}) collective-permute-start(f32[192,256]{1,0:T(8,128)S(1)} %get-tuple-element.20), channel_id=1, source_target_pairs={{0,8},{1,16},{2,24},{3,0},{4,9},{5,17},{6,25},{7,1},{8,10},{9,18},... | collective-permute-start | bytes 589832 | tf_op jit(solution)/shard_map/ppermute | solution.py:37
  22.0 79.3 %collective-permute-start.6 = (f32[192,256]{1,0:T(8,128)S(1)}, f32[192,256]{1,0:T(8,128)S(1)}, u32[]{:S(2)}, u32[]{:S(2)}) collective-permute-start(f32[192,256]{1,0:T(8,128)S(1)} %get-tuple-element.19), channel_id=1, source_target_pairs={{0,16},{1,24},{2,0},{3,8},{4,17},{5,25},{6,1},{7,9},{8,18},{9,26},... | collective-permute-start | bytes 589832 | tf_op jit(solution)/shard_map/ppermute | solution.py:37
  24.0 79.2 %collective-permute-start.7 = (f32[192,256]{1,0:T(8,128)S(1)}, f32[192,256]{1,0:T(8,128)S(1)}, u32[]{:S(2)}, u32[]{:S(2)}) collective-permute-start(f32[192,256]{1,0:T(8,128)S(1)} %get-tuple-element.18), channel_id=1, source_target_pairs={{0,24},{1,0},{2,8},{3,16},{4,25},{5,1},{6,9},{7,17},{8,26},{9,2},{... | collective-permute-start | bytes 589832 | tf_op jit(solution)/shard_map/ppermute | solution.py:37
  31.0 75.7 %collective-permute-start = (f32[192,256]{1,0:T(8,128)}, f32[192,256]{1,0:T(8,128)}, u32[]{:S(2)}, u32[]{:S(2)}) collective-permute-start(f32[192,256]{1,0:T(8,128)} %get-tuple-element.13), channel_id=1, source_target_pairs={{0,0},{1,8},{2,16},{3,24},{4,1},{5,9},{6,17},{7,25},{8,2},{9,10},{... | collective-permute-start | bytes 589832 | tf_op jit(solution)/shard_map/ppermute | solution.py:37
  34.1 80.0 %collective-permute-start.1 = (f32[192,256]{1,0:T(8,128)}, f32[192,256]{1,0:T(8,128)}, u32[]{:S(2)}, u32[]{:S(2)}) collective-permute-start(f32[192,256]{1,0:T(8,128)} %get-tuple-element.16), channel_id=1, source_target_pairs={{0,8},{1,16},{2,24},{3,0},{4,9},{5,17},{6,25},{7,1},{8,10},{9,18},... | collective-permute-start | bytes 589832 | tf_op jit(solution)/shard_map/ppermute | solution.py:37
  84.5 33.8 %collective-permute-start.2 = (f32[192,256]{1,0:T(8,128)S(1)}, f32[192,256]{1,0:T(8,128)}, u32[]{:S(2)}, u32[]{:S(2)}) collective-permute-start(f32[192,256]{1,0:T(8,128)S(1)} %get-tuple-element.15), channel_id=1, source_target_pairs={{0,16},{1,24},{2,0},{3,8},{4,17},{5,25},{6,1},{7,9},{8,18},{9,26},... | collective-permute-start | bytes 589832 | tf_op jit(solution)/shard_map/ppermute | solution.py:37
  101.3 17.0 %collective-permute-start.3 = (f32[192,256]{1,0:T(8,128)S(1)}, f32[192,256]{1,0:T(8,128)}, u32[]{:S(2)}, u32[]{:S(2)}) collective-permute-start(f32[192,256]{1,0:T(8,128)S(1)} %get-tuple-element.14), channel_id=1, source_target_pairs={{0,24},{1,0},{2,8},{3,16},{4,25},{5,1},{6,9},{7,17},{8,26},{9,2},{... | collective-permute-start | bytes 589832 | tf_op jit(solution)/shard_map/ppermute | solution.py:37
  125.9 121.1 %all-gather.7.cloned.1.call-start = ((), (), s32[]{:S(2)}) async-start(), calls=%async_computation.6 | async-start | bytes 3932160 | tf_op jit(solution)/shard_map/all_gather | solution.py:40
  126.6 194.4 %reduce-scatter.3.cloned.1.call-start = ((), (), s32[]{:S(2)}) async-start(), calls=%async_computation.2 | async-start | bytes 7077888 | tf_op jit(solution)/shard_map/reduce_scatter | solution.py:45
  246.9 143.7 %reduce-scatter.5.cloned.1.call-start = ((), (), s32[]{:S(2)}) async-start(), calls=%async_computation.3 | async-start | bytes 7077888 | tf_op jit(solution)/shard_map/reduce_scatter | solution.py:45
  320.7 204.3 %all-reduce.2.cloned.1.call-start = ((), (), s32[]{:S(2)}) async-start(), calls=%async_computation.4 | async-start | bytes 1048576 | tf_op jit(solution)/shard_map/psum | solution.py:49
  391.8 0.9 copy-start.1
Sparse Core Ops, SparseCore 0:
  126.0 47.1 all-gather.4
  175.0 43.8 all-gather.6
  247.0 69.6 reduce-scatter.2
  320.8 69.7 reduce-scatter.4
  397.4 127.5 all-reduce.1
